TPU v7x, 32 devices: a whole 2x2x4 slice. The times are simulated.
32 devices in a mesh: row: 8 (over y, x, core), col: 4 (over z).
Axes of the slice: x: 2, y: 2, z: 4, core: 2. Of those that a mesh axis runs over, the one named last changes fastest.
Arguments:
- descriptors: bfloat16 [32, 6144], P(None, ('row', 'col')), may hold values from -6 to 6
- densities: float32 [6144], P(('row', 'col')), may hold values from 0.25 to 4
- vectors: float32 [32, 6144], P(None, ('row', 'col')), may hold values from -6 to 6
Outputs:
- next_block: float32 [32, 6144], P(None, ('row', 'col'))
All inputs are finite; a program needn't handle non-finite values.
Results may differ from a plain program's by a relative error of at most 0.0036.
Values may be sent and summed in bfloat16 or wider, within the bound.
No kernel may reach another device: no remote copies, remote signals or barrier semaphores. Data moves between devices by JAX's collectives and lax.ppermute only.
A program may use at most 64 MiB of HBM per device.

v0:
```python
import math
import jax
import jax.numpy as jnp
from jax import lax
from jax.sharding import PartitionSpec as P

kernel_width = 8.0


def tile_terms(targets, target_norm, piece):
    piece_feat, piece_vals, piece_inv = piece
    piece_norm = jnp.sum(jnp.square(piece_feat.astype(jnp.float32)), axis=0)
    feature_dim, target_count = targets.shape
    span_rows = math.gcd(target_count, 512)
    block_count = target_count // span_rows
    blocks = targets.reshape(feature_dim, block_count, span_rows).transpose(1, 0, 2)
    norm_blocks = target_norm.reshape(block_count, span_rows)

    def tile_block(block_item):
        block_feat, block_norm = block_item
        inner_prod = lax.dot_general(
            block_feat, piece_feat, (((0,), (0,)), ((), ())), preferred_element_type=jnp.float32
        )
        kernel = jnp.exp(
            -(block_norm[:, None] + piece_norm[None, :] - 2.0 * inner_prod) / kernel_width
        ).astype(jnp.bfloat16)
        numerator = lax.dot_general(
            piece_vals, kernel, (((1,), (1,)), ((), ())), preferred_element_type=jnp.float32
        )
        degree = lax.dot_general(
            piece_inv, kernel, (((1,), (1,)), ((), ())), preferred_element_type=jnp.float32
        )
        return (numerator, degree)

    numerator, degree = lax.map(tile_block, (blocks, norm_blocks))
    numerator = numerator.transpose(1, 0, 2).reshape(piece_vals.shape[0], target_count)
    degree = degree.transpose(1, 0, 2).reshape(1, target_count)
    return (numerator, degree)


def accumulate(targets, vec_count):
    target_norm = jnp.sum(jnp.square(targets.astype(jnp.float32)), axis=0)

    def fold_piece(running, piece, start):
        numerator, degree = tile_terms(targets, target_norm, piece)
        return (numerator, degree)

    initial = (
        jnp.zeros((vec_count, targets.shape[1]), jnp.float32),
        jnp.zeros((1, targets.shape[1]), jnp.float32),
    )
    return (fold_piece, initial)


def per_device(descriptors, densities, vectors):
    highest = lax.Precision.HIGHEST
    vec_count = vectors.shape[0]
    weighted = (vectors / densities[None, :]).astype(jnp.bfloat16)
    inverse = (1.0 / densities).astype(jnp.bfloat16)[None, :]
    targets = lax.all_gather(descriptors, "col", axis=1, tiled=True)
    fold_piece, initial = accumulate(targets, vec_count)
    partial_value = fold_piece(
        initial,
        (
            lax.all_gather(descriptors, "row", axis=1, tiled=True),
            lax.all_gather(weighted, "row", axis=1, tiled=True),
            lax.all_gather(inverse, "row", axis=1, tiled=True),
        ),
        jnp.int32(0),
    )
    numerator, degree = (
        lax.psum_scatter(partial_value[0], "col", scatter_dimension=1, tiled=True),
        lax.psum_scatter(partial_value[1], "col", scatter_dimension=1, tiled=True),
    )
    diffused = numerator / degree
    samples_float = float(descriptors.shape[1] * lax.axis_size("row") * lax.axis_size("col"))
    coupling, diffused_gram, basis_gram = lax.psum(
        (
            jnp.dot(vectors, diffused.T, precision=highest),
            jnp.dot(diffused, diffused.T, precision=highest),
            jnp.dot(vectors, vectors.T, precision=highest),
        ),
        ("row", "col"),
    )
    remainder = diffused - jnp.dot(coupling.T, vectors, precision=highest) / samples_float
    cross_term = jnp.dot(coupling.T, coupling, precision=highest)
    basis_term = jnp.dot(
        coupling.T, jnp.dot(basis_gram, coupling, precision=highest), precision=highest
    )
    spread = (
        diffused_gram
        - 2.0 * cross_term / samples_float
        + basis_term / (samples_float * samples_float)
    )
    factor = jnp.linalg.cholesky(spread)
    solved = jax.scipy.linalg.solve_triangular(factor, remainder, lower=True)
    return math.sqrt(samples_float) * solved


def solution(mesh):
    return jax.shard_map(
        per_device,
        mesh=mesh,
        in_specs=(P(None, ("row", "col")), P(("row", "col")), P(None, ("row", "col"))),
        out_specs=P(None, ("row", "col")),
        check_vma=False,
    )
```

profile of v0, /device:TPU:0, one launch (start us, length us, event | category | flops | bytes accessed | tf_op | source)
XLA Modules:
  0.0 157.3 jit_solution(3891402411580507994)
XLA Ops:
  6.5 11.0 %all-gather.2 = bf16[8,192,32]{1,2,0:T(8,128)(2,1)S(1)} all-gather(bf16[1,192,32]{1,2,0:T(8,128)(2,1)} %bitcast.102), channel_id=1, replica_groups=mesh['row'=8,'col'=4] {'row'}, dimensions={0}, use_global_device_ids=true | all-gather | bytes 110592 | tf_op jit(solution)/shard_map/all_gather | solution.py:65
  17.5 13.6 %all-gather.1 = bf16[4,192,32]{1,2,0:T(8,128)(2,1)S(1)} all-gather(bf16[1,192,32]{1,2,0:T(8,128)(2,1)} %bitcast.103), channel_id=1, replica_groups=mesh['row'=8,'col'=4] {'col'}, dimensions={0}, use_global_device_ids=true | all-gather | bytes 61440 | tf_op jit(solution)/shard_map/all_gather | solution.py:60
  31.7 9.0 %all-gather.3 = bf16[8,192,32]{1,2,0:T(8,128)(2,1)S(1)} all-gather(bf16[1,192,32]{1,2,0:T(8,128)(2,1)S(1)} %fusion.17), channel_id=1, replica_groups=mesh['row'=8,'col'=4] {'row'}, dimensions={0}, use_global_device_ids=true | all-gather | bytes 110592 | tf_op jit(solution)/shard_map/all_gather | solution.py:66
  40.9 0.6 dynamic-slice
  42.4 13.2 %all-reduce = bf16[1536]{0:T(1024)(128)(2,1)S(1)} all-reduce(bf16[1536]{0:T(1024)(128)(2,1)S(1)} %dynamic-update-slice.3), channel_id=2, replica_groups=mesh['row'=8,'col'=4] {'row'}, use_global_device_ids=true, to_apply=%add | all-reduce | flops 1536 | bytes 6144
  55.6 3.6 %while.12 = (s32[]{:T(128)}, f32[3,32,256]{2,1,0:T(8,128)S(1)}, f32[3,1,256]{2,1,0:T(1,128)S(1)}, f32[3,256]{1,0:T(4,128)S(1)}, f32[1536]{0:T(1024)S(1)}, /*inde...) while((s32[]{:T(128)}, f32[3,32,256]{2,1,0:T(8,128)S(1)}, ...), condition=%wide.region_3.4_spmd, body=%wide.region_2.3_spmd.sunk | while | flops 53477376 | bytes 2623605 | solution.py:35
  55.7 0.5 fusion.52
  56.5 0.3 fusion.54
  56.8 0.6 fusion.52
  57.7 0.3 fusion.54
  58.0 0.6 fusion.52
  58.9 0.3 fusion.54
  59.2 1.0 copy.40
  60.3 0.9 copy.42
  61.4 19.1 %reduce-scatter.9.cloned.1.call-done = f32[192,1]{1,0:T(8,128)} async-done(((f32[768,1]{1,0:T(8,128)}), f32[192,1]{1,0:T(8,128)}) %reduce-scatter.9.cloned.1.call-update) | async-done | bytes 784
  80.4 1.0 copy.41
  81.4 20.4 %reduce-scatter.7.cloned.1.call-done = f32[192,32]{1,0:T(8,128)} async-done(((f32[768,32]{1,0:T(8,128)}), f32[192,32]{1,0:T(8,128)}) %reduce-scatter.7.cloned.1.call-update) | async-done | bytes 24592
  101.8 1.0 copy.39
  103.1 39.0 %all-reduce.1 = (f32[32,32]{0,1:T(8,128)S(1)}, f32[32,32]{0,1:T(8,128)S(1)}, f32[32,32]{1,0:T(8,128)S(1)}) all-reduce(f32[32,32]{0,1:T(8,128)S(1)} %convolution_bitcast_fusion.2, f32[32,32]{0,1:T(8,128)S(1)} %fusion.18, f32[32,32]{1,0:T(8,128)S(1)} %fusion.19), channel_id=1, replica_groups=mesh['row'=8,'col'=4] {'row','col'}, use_global_device_ids=true, to_apply=%region_7.8 | all-reduce | flops 3072 | bytes 24576 | tf_op jit(solution)/shard_map/psum | solution.py:77
  142.9 2.9 %cholesky.16 = f32[32,32]{1,0:T(8,128)S(1)} custom-call(f32[32,32]{1,0:T(8,128)S(1)} %fusion.16), custom_call_target="Cholesky" | custom-call | tf_op jit(solution)/shard_map/jit(cholesky)/cholesky | solution.py:95
  145.8 0.6 compare_reduce_fusion
  146.5 0.7 fusion.14
  147.1 2.4 %custom-call.7 = f32[1,32,32]{1,2,0:T(8,128)S(1)} custom-call(f32[1,32,32]{2,1,0:T(8,128)S(1)} %fusion.14), custom_call_target="InvertDiagBlocksLowerTriangular" | custom-call | tf_op jit(solution)/shard_map/jit(_solve_triangular)/triangular_solve | solution.py:96
  149.6 0.9 convolution_multiply_fusion.1
  (44 shorter events, 3.3 us)
Async XLA Ops:
  6.5 25.1 %copy-start.1 = (f32[192]{0:T(256)S(1)}, f32[192]{0:T(256)}, u32[]{:S(2)}) copy-start(f32[192]{0:T(256)} %param.6) | copy-start | bytes 2308
  6.5 25.1 %copy-start = (f32[32,192]{1,0:T(8,128)S(1)}, f32[32,192]{1,0:T(8,128)}, u32[]{:S(2)}) copy-start(f32[32,192]{1,0:T(8,128)} %param.7) | copy-start | bytes 73732
  6.5 73.9 %reduce-scatter.9.cloned.1.call-start = ((), (), s32[]{:S(2)}) async-start(), calls=%async_computation.3 | async-start | bytes 491520
  31.2 9.8 %copy-start.2 = (u32[32]{0:T(128)S(1)}, u32[32]{0:T(128)}, u32[]{:S(2)}) copy-start(u32[32]{0:T(128)} %constant.83) | copy-start | bytes 388
  60.2 41.6 %reduce-scatter.7.cloned.1.call-start = ((), (), s32[]{:S(2)}) async-start(), calls=%async_computation.2 | async-start | bytes 491520
Sparse Core Ops, SparseCore 0:
  60.3 20.0 reduce-scatter.8
  82.7 19.0 reduce-scatter.6
where the time goes:
time: 158 us; the launch traced here: 157 us
  blocking collectives  85.7 us (54%)
  waiting for transfers between devices  39.5 us (25%)
  between operations  14.2 us (9%)
  other arithmetic  6.76 us (4%)
  matrix products  5.55 us (4%)
  local copies, waits for them, and re-layouts  5.41 us (3%)
    unnamed x4, waiting for transfers between devices  39.5 us
    psum x1, blocking collectives, per_device(): lax.psum((jnp.dot(vectors, diffused.T, precision=highest), jnp.dot(diffus...  39 us
    all_gather x1, blocking collectives, per_device(): targets = lax.all_gather(descriptors, 'col', axis=1, tiled=True)  13.6 us
    unnamed x1, blocking collectives  13.2 us
    all_gather x1, blocking collectives, per_device(): lax.all_gather(descriptors, 'row', axis=1, tiled=True)  11 us
    all_gather x1, blocking collectives, per_device(): lax.all_gather(weighted, 'row', axis=1, tiled=True)  9.01 us
    unnamed x16, local copies, waits for them, and re-layouts  5.06 us
    another operation x3, other arithmetic, per_device(): factor = jnp.linalg.cholesky(spread)  3.6 us
  transfers between devices with their start and end apart: 2, of which 2 were waited for; matrix products, arithmetic and copies ran while one was open for 1% of the time, Pallas kernels for 0%

commit v1 on v0

--- a/solution.py
+++ b/solution.py
@@ -5,6 +5,17 @@
 from jax.sharding import PartitionSpec as P
 
 kernel_width = 8.0
+
+
+def around_the_ring(x, mesh_axis, along):
+    size = lax.axis_size(mesh_axis)
+    route = [(i, (i + 1) % size) for i in range(size)]
+    terms = [x]
+    for far in range(1, size):
+        terms = [lax.ppermute(terms[0], mesh_axis, route), *terms]
+    whole = jnp.concatenate(terms, axis=along)
+    shift = (lax.axis_index(mesh_axis) + 1) * terms[-1].shape[along]
+    return jnp.roll(whole, shift, axis=along)
 
 
 def tile_terms(targets, target_norm, piece):
@@ -57,7 +68,7 @@
     vec_count = vectors.shape[0]
     weighted = (vectors / densities[None, :]).astype(jnp.bfloat16)
     inverse = (1.0 / densities).astype(jnp.bfloat16)[None, :]
-    targets = lax.all_gather(descriptors, "col", axis=1, tiled=True)
+    targets = around_the_ring(descriptors, "col", 1)
     fold_piece, initial = accumulate(targets, vec_count)
     partial_value = fold_piece(
         initial,

time: 158 us -> 150 us (0.949)
  blocking collectives: 85.7 us -> 70.2 us
  starting transfers between devices: 0.04 us -> 6.35 us
    all_gather x1 -> x0, blocking collectives: 13.6 us -> none  [per_device(): targets = lax.all_gather(descriptors, 'col', axis=1, tiled=True)]
    ppermute x0 -> x3, starting transfers between devices: none -> 6.31 us  [around_the_ring(): terms = [lax.ppermute(terms[0], mesh_axis, route), *terms]]
    all_gather x1, blocking collectives: 11 us -> 9.38 us  [per_device(): lax.all_gather(descriptors, 'row', axis=1, tiled=True)]
    unnamed x16 -> x15, local copies, waits for them, and re-layouts: 5.06 us -> 5.03 us
  transfers between devices with their start and end apart: 2 -> 5, of which waited for: 2 -> 2; matrix products, arithmetic and copies ran while one was open for 1% -> 3% of each run, Pallas kernels for 0% -> 0%
where the time goes in v1:
time: 150 us; the launch traced here: 149 us
  blocking collectives  70.2 us (47%)
  waiting for transfers between devices  39.1 us (26%)
  between operations  14.3 us (10%)
  other arithmetic  8.28 us (6%)
  starting transfers between devices  6.35 us (4%)
  matrix products  5.55 us (4%)
  local copies, waits for them, and re-layouts  5.43 us (4%)
    unnamed x4, waiting for transfers between devices  39.1 us
    psum x1, blocking collectives, per_device(): lax.psum((jnp.dot(vectors, diffused.T, precision=highest), jnp.dot(diffus...  38.9 us
    unnamed x1, blocking collectives  12.9 us
    all_gather x1, blocking collectives, per_device(): lax.all_gather(descriptors, 'row', axis=1, tiled=True)  9.38 us
    all_gather x1, blocking collectives, per_device(): lax.all_gather(weighted, 'row', axis=1, tiled=True)  9.02 us
    ppermute x3, starting transfers between devices, around_the_ring(): terms = [lax.ppermute(terms[0], mesh_axis, route), *terms]  6.31 us
    unnamed x15, local copies, waits for them, and re-layouts  5.03 us
    another operation x3, other arithmetic, per_device(): factor = jnp.linalg.cholesky(spread)  3.6 us
  transfers between devices with their start and end apart: 5, of which 2 were waited for; matrix products, arithmetic and copies ran while one was open for 3% of the time, Pallas kernels for 0%

profile of v1, /device:TPU:0, one launch (start us, length us, event | category | flops | bytes accessed | tf_op | source)
XLA Modules:
  0.0 149.3 jit_solution(5756020107649181584)
XLA Ops:
  6.5 3.1 %collective-permute-start = (bf16[32,192]{1,0:T(8,128)(2,1)}, bf16[32,192]{1,0:T(8,128)(2,1)S(1)}, u32[]{:S(2)}, u32[]{:S(2)}) collective-permute-start(bf16[32,192]{1,0:T(8,128)(2,1)} %param.5), channel_id=1, source_target_pairs={{0,1},{1,2},{2,3},{3,0},{4,5},{5,6},{6,7},{7,4},{8,9},{9,10},{10,1... | collective-permute-start | bytes 36872 | tf_op jit(solution)/shard_map/ppermute | solution.py:15
  9.6 0.7 divide_convert_fusion.1
  10.3 0.8 fusion.17
  11.0 9.4 %all-gather.1 = bf16[8,192,32]{1,2,0:T(8,128)(2,1)S(1)} all-gather(bf16[1,192,32]{1,2,0:T(8,128)(2,1)} %bitcast.94), channel_id=1, replica_groups=mesh['row'=8,'col'=4] {'row'}, dimensions={0}, use_global_device_ids=true | all-gather | bytes 110592 | tf_op jit(solution)/shard_map/all_gather | solution.py:76
  20.7 1.6 %collective-permute-start.1 = (bf16[32,192]{1,0:T(8,128)(2,1)S(1)}, bf16[32,192]{1,0:T(8,128)(2,1)S(1)}, u32[]{:S(2)}, u32[]{:S(2)}) collective-permute-start(bf16[32,192]{1,0:T(8,128)(2,1)S(1)} %collective-permute-done), channel_id=1, source_target_pairs={{0,1},{1,2},{2,3},{3,0},{4,5},{5,6},{6,7},{7,4},{8,9},{9,10},{10,1... | collective-permute-start | bytes 36872 | tf_op jit(solution)/shard_map/ppermute | solution.py:15
  22.4 0.7 dynamic-slice
  24.0 12.9 %all-reduce = bf16[1536]{0:T(1024)(128)(2,1)S(1)} all-reduce(bf16[1536]{0:T(1024)(128)(2,1)S(1)} %dynamic-update-slice.3), channel_id=2, replica_groups=mesh['row'=8,'col'=4] {'row'}, use_global_device_ids=true, to_apply=%add | all-reduce | flops 1536 | bytes 6144
  37.0 1.6 %collective-permute-start.2 = (bf16[32,192]{1,0:T(8,128)(2,1)S(1)}, bf16[32,192]{1,0:T(8,128)(2,1)S(1)}, u32[]{:S(2)}, u32[]{:S(2)}) collective-permute-start(bf16[32,192]{1,0:T(8,128)(2,1)S(1)} %collective-permute-done.1), channel_id=1, source_target_pairs={{0,1},{1,2},{2,3},{3,0},{4,5},{5,6},{6,7},{7,4},{8,9},{9,10},{10,1... | collective-permute-start | bytes 36872 | tf_op jit(solution)/shard_map/ppermute | solution.py:15
  38.6 9.0 %all-gather.2 = bf16[8,192,32]{1,2,0:T(8,128)(2,1)S(1)} all-gather(bf16[1,192,32]{1,2,0:T(8,128)(2,1)S(1)} %fusion.17), channel_id=1, replica_groups=mesh['row'=8,'col'=4] {'row'}, dimensions={0}, use_global_device_ids=true | all-gather | bytes 110592 | tf_op jit(solution)/shard_map/all_gather | solution.py:77
  48.1 3.6 %while.12 = (s32[]{:T(128)}, f32[3,32,256]{2,1,0:T(8,128)S(1)}, f32[3,1,256]{2,1,0:T(1,128)S(1)}, f32[3,256]{1,0:T(4,128)S(1)}, f32[1536]{0:T(1024)S(1)}, /*inde...) while((s32[]{:T(128)}, f32[3,32,256]{2,1,0:T(8,128)S(1)}, ...), condition=%wide.region_3.4_spmd, body=%wide.region_2.3_spmd.sunk | while | flops 53477376 | bytes 2623605 | solution.py:46
  49.3 0.6 fusion.52
  50.5 0.6 fusion.52
  51.7 1.0 copy.37
  52.8 0.9 copy.39
  53.9 18.6 %reduce-scatter.9.cloned.1.call-done = f32[192,1]{1,0:T(8,128)} async-done(((f32[768,1]{1,0:T(8,128)}), f32[192,1]{1,0:T(8,128)}) %reduce-scatter.9.cloned.1.call-update) | async-done | bytes 784
  72.5 1.0 copy.38
  73.5 20.4 %reduce-scatter.7.cloned.1.call-done = f32[192,32]{1,0:T(8,128)} async-done(((f32[768,32]{1,0:T(8,128)}), f32[192,32]{1,0:T(8,128)}) %reduce-scatter.7.cloned.1.call-update) | async-done | bytes 24592
  93.9 1.0 copy.36
  95.2 38.9 %all-reduce.1 = (f32[32,32]{0,1:T(8,128)S(1)}, f32[32,32]{0,1:T(8,128)S(1)}, f32[32,32]{1,0:T(8,128)S(1)}) all-reduce(f32[32,32]{0,1:T(8,128)S(1)} %convolution_bitcast_fusion.2, f32[32,32]{0,1:T(8,128)S(1)} %fusion.18, f32[32,32]{1,0:T(8,128)S(1)} %fusion.19), channel_id=1, replica_groups=mesh['row'=8,'col'=4] {'row','col'}, use_global_device_ids=true, to_apply=%region_7.8 | all-reduce | flops 3072 | bytes 24576 | tf_op jit(solution)/shard_map/psum | solution.py:88
  134.9 2.9 %cholesky.16 = f32[32,32]{1,0:T(8,128)S(1)} custom-call(f32[32,32]{1,0:T(8,128)S(1)} %fusion.16), custom_call_target="Cholesky" | custom-call | tf_op jit(solution)/shard_map/jit(cholesky)/cholesky | solution.py:106
  137.9 0.6 compare_reduce_fusion
  138.5 0.7 fusion.14
  139.2 2.4 %custom-call.7 = f32[1,32,32]{1,2,0:T(8,128)S(1)} custom-call(f32[1,32,32]{2,1,0:T(8,128)S(1)} %fusion.14), custom_call_target="InvertDiagBlocksLowerTriangular" | custom-call | tf_op jit(solution)/shard_map/jit(_solve_triangular)/triangular_solve | solution.py:107
  141.6 0.9 convolution_multiply_fusion.1
  (48 shorter events, 4.8 us)
Async XLA Ops:
  6.5 15.9 %copy-start.2 = (u32[32]{0:T(128)S(1)}, u32[32]{0:T(128)}, u32[]{:S(2)}) copy-start(u32[32]{0:T(128)} %constant.109) | copy-start | bytes 388
  6.5 41.3 %copy-start.1 = (bf16[32,192]{1,0:T(8,128)(2,1)S(1)}, bf16[32,192]{1,0:T(8,128)(2,1)}, u32[]{:S(2)}) copy-start(bf16[32,192]{1,0:T(8,128)(2,1)} %param.5) | copy-start | bytes 36868
  6.5 66.0 %reduce-scatter.9.cloned.1.call-start = ((), (), s32[]{:S(2)}) async-start(), calls=%async_computation.3 | async-start | bytes 491520
  6.5 14.1 %collective-permute-start = (bf16[32,192]{1,0:T(8,128)(2,1)}, bf16[32,192]{1,0:T(8,128)(2,1)S(1)}, u32[]{:S(2)}, u32[]{:S(2)}) collective-permute-start(bf16[32,192]{1,0:T(8,128)(2,1)} %param.5), channel_id=1, source_target_pairs={{0,1},{1,2},{2,3},{3,0},{4,5},{5,6},{6,7},{7,4},{8,9},{9,10},{10,1... | collective-permute-start | bytes 36872 | tf_op jit(solution)/shard_map/ppermute | solution.py:15
  20.7 16.3 %collective-permute-start.1 = (bf16[32,192]{1,0:T(8,128)(2,1)S(1)}, bf16[32,192]{1,0:T(8,128)(2,1)S(1)}, u32[]{:S(2)}, u32[]{:S(2)}) collective-permute-start(bf16[32,192]{1,0:T(8,128)(2,1)S(1)} %collective-permute-done), channel_id=1, source_target_pairs={{0,1},{1,2},{2,3},{3,0},{4,5},{5,6},{6,7},{7,4},{8,9},{9,10},{10,1... | collective-permute-start | bytes 36872 | tf_op jit(solution)/shard_map/ppermute | solution.py:15
  37.0 10.9 %collective-permute-start.2 = (bf16[32,192]{1,0:T(8,128)(2,1)S(1)}, bf16[32,192]{1,0:T(8,128)(2,1)S(1)}, u32[]{:S(2)}, u32[]{:S(2)}) collective-permute-start(bf16[32,192]{1,0:T(8,128)(2,1)S(1)} %collective-permute-done.1), channel_id=1, source_target_pairs={{0,1},{1,2},{2,3},{3,0},{4,5},{5,6},{6,7},{7,4},{8,9},{9,10},{10,1... | collective-permute-start | bytes 36872 | tf_op jit(solution)/shard_map/ppermute | solution.py:15
  51.7 2.0 %copy-start = (f32[32,192]{1,0:T(8,128)S(1)}, f32[32,192]{1,0:T(8,128)}, u32[]{:S(2)}) copy-start(f32[32,192]{1,0:T(8,128)} %param.7) | copy-start | bytes 73732
  52.7 41.2 %reduce-scatter.7.cloned.1.call-start = ((), (), s32[]{:S(2)}) async-start(), calls=%async_computation.2 | async-start | bytes 491520
Sparse Core Ops, SparseCore 0:
  52.8 19.6 reduce-scatter.8
  74.8 19.0 reduce-scatter.6
